TPU v7x, 128 devices: a whole 4x4x4 slice. The times are simulated.
128 devices in a mesh: row: 8 (over x, core), col: 16 (over z, y).
Axes of the slice: x: 4, y: 4, z: 4, core: 2. Of those that a mesh axis runs over, the one named last changes fastest.
Arguments:
- tiles: bfloat16 [8, 16, 384, 128, 128], P('row', 'col'), may hold values from -0.15625 to 0.15625
- tile_row: int32 [8, 16, 384], P('row', 'col'), may hold values from 0 to 511, as said below
- tile_col: int32 [8, 16, 384], P('row', 'col'), may hold values from 0 to 255
- tile_count: int32 [8, 16], P('row', 'col'), may hold values from 96 to 384, as said below
- vectors: bfloat16 [32, 8, 16, 4096], P(None, 'row', 'col'), may hold values from -6 to 6
Outputs:
- image: bfloat16 [32, 524288], P(None, ('row', 'col'))
- back_image: bfloat16 [32, 8, 16, 4096], P(None, 'row', 'col')
Inputs may be any that keep to these rules, and one draw needn't show every extreme that they name: `tile_count`: some device has exactly 384 live slots. `tile_row`: the slots of each device, live or not, name exactly 12 distinct block rows in each aligned run of 32 block rows.
All inputs are finite; a program needn't handle non-finite values.
Results may differ from a plain program's by a relative error of at most 0.0041.
Values may be sent and summed in bfloat16 or wider, within the bound.
No kernel may reach another device: no remote copies, remote signals or barrier semaphores. Data moves between devices by JAX's collectives and lax.ppermute only.
A program may use at most 128 MiB of HBM per device.

v0:
```python
import jax
import jax.numpy as jnp
from jax import lax
from jax.sharding import PartitionSpec as P


def per_device(tiles, tile_row, tile_col, tile_count, vectors):
    vec_cols = vectors.shape[0]
    tile_size = tiles.shape[-1]
    slot_count = tiles.shape[2]
    local_tiles = tiles[0, 0]
    rows_local = tile_row[0, 0]
    cols_local = tile_col[0, 0]
    live_count = tile_count[0, 0]
    live_mask = (jnp.arange(slot_count, dtype=jnp.int32) < live_count).astype(jnp.float32)
    row_devices = lax.axis_size("row")
    col_devices = lax.axis_size("col")
    gathered = lax.all_gather(vectors, "row", axis=1, tiled=True)
    blk_cols = gathered.shape[1] * gathered.shape[3] // tile_size
    blk_rows = blk_cols * col_devices // row_devices
    col_vectors = gathered.reshape(vec_cols, blk_cols, tile_size)

    def slot_group():
        return (local_tiles, rows_local, cols_local, live_mask)

    def forward_terms(totals, start_slot, group_size):
        tile_block, row_index, col_index, slot_mask = slot_group()
        picked = jnp.take(col_vectors, col_index, axis=1)
        product = jnp.einsum("ksj,sij->ksi", picked, tile_block, preferred_element_type=jnp.float32)
        return totals.at[:, row_index].add(product * slot_mask[None, :, None])

    def sweep(term_fn, totals_zero):
        return term_fn(totals_zero, 0, slot_count)

    forward_sum = sweep(forward_terms, jnp.zeros((vec_cols, blk_rows, tile_size), jnp.float32))
    partial_rows = forward_sum.reshape(vec_cols, blk_rows * tile_size)
    share_sum = lax.psum_scatter(partial_rows, "col", scatter_dimension=1, tiled=True)
    image = share_sum.astype(jnp.bfloat16)
    row_image = lax.all_gather(image, "col", axis=1, tiled=True)
    row_blocks = row_image.reshape(vec_cols, blk_rows, tile_size)

    def backward_terms(totals, start_slot, group_size):
        tile_block, row_index, col_index, slot_mask = slot_group()
        picked = jnp.take(row_blocks, row_index, axis=1)
        product = jnp.einsum("ksi,sij->ksj", picked, tile_block, preferred_element_type=jnp.float32)
        return totals.at[:, col_index].add(product * slot_mask[None, :, None])

    backward_sum = sweep(backward_terms, jnp.zeros((vec_cols, blk_cols, tile_size), jnp.float32))
    partial_cols = backward_sum.reshape(vec_cols, row_devices, 1, vectors.shape[3])
    back_sum = lax.psum_scatter(partial_cols, "row", scatter_dimension=1, tiled=True)
    return (image, back_sum.astype(jnp.bfloat16))


def solution(mesh):
    return jax.shard_map(
        per_device,
        mesh=mesh,
        in_specs=(
            P("row", "col", None, None, None),
            P("row", "col", None),
            P("row", "col", None),
            P("row", "col"),
            P(None, "row", "col", None),
        ),
        out_specs=(P(None, ("row", "col")), P(None, "row", "col", None)),
        check_vma=False,
    )
```

profile of v0, /device:TPU:0, one launch (start us, length us, event | category | flops | bytes accessed | tf_op | source)
XLA Modules:
  0.0 400.8 jit_solution(5015955300966419793)
XLA Ops:
  7.2 0.0 all-gather.3.cloned.1.call-start
  7.2 0.7 all-gather.3.cloned.1.call-update
  7.9 0.0 reduce-scatter.3.cloned.1.call-start
  8.6 0.7 reduce.1
  9.3 0.7 fusion.22
  10.0 0.7 fusion.21
  10.7 26.6 %all-gather.3.cloned.1.call-done = bf16[32,8,1,4096]{3,0,2,1:T(8,128)(2,1)} async-done(((bf16[32,1,1,4096]{3,0,2,1:T(8,128)(2,1)}), bf16[32,8,1,4096]{3,0,2,1:T(8,128)(2,1)}) %all-gather.3.cloned.1.call-update) | async-done | bytes 2097168 | tf_op jit(solution)/shard_map/all_gather | solution.py:18
  37.3 2.7 copy.18
  40.1 2.4 reshape.89
  42.5 2.9 copy.19
  45.4 3.2 gather_fusion
  48.6 14.9 %broadcast_multiply_fusion.1 = f32[384,32,128]{2,1,0:T(8,128)} fusion(f32[384]{0:T(512)S(1)} %get-tuple-element.6, bf16[1,1,384,128,128]{4,3,2,1,0:T(8,128)(2,1)} %param.5, bf16[384,32,128]{2,1,0:T(8,128)(2,1)} %gather_fusion, pred[384]{0:T(512)(128)(4,1)S(1)} %get-tuple-element.7), kind=kOutput, calls=%fused_computation.15 | convolution fusion | flops 405798912 | bytes 22022016 | tf_op jit(solution)/shard_map/ksj,sij->ksi/dot_general | solution.py:29
  63.5 4.3 %broadcast_in_dim.28 = f32[32,512,128]{2,0,1:T(8,128)} broadcast(f32[]{:T(128)} %constant.18.clone.1), dimensions={} | broadcast | bytes 8388612 | tf_op jit(solution)/shard_map/broadcast_in_dim | solution.py:35
  67.8 51.2 %scatter_fusion = f32[32,512,128]{2,0,1:T(8,128)} fusion(f32[32,512,128]{2,0,1:T(8,128)} %broadcast_in_dim.28, s32[384]{0:T(512)S(1)} %fusion.21, f32[384,32,128]{2,1,0:T(8,128)} %broadcast_multiply_fusion.1), kind=kCustom, calls=%fused_computation.2 | custom fusion | flops 1572864 | bytes 18875904 | tf_op jit(solution)/shard_map/scatter-add | solution.py:30
  119.1 7.1 %copy_bitcast_fusion = f32[32,65536]{1,0:T(8,128)} fusion(f32[32,512,128]{2,0,1:T(8,128)} %scatter_fusion), kind=kLoop, calls=%fused_computation.8 | loop fusion | bytes 16777216 | tf_op jit(solution)/shard_map/reshape | solution.py:36
  126.2 0.0 reduce-scatter.3.cloned.1.call-update
  126.2 0.0 all-gather.5.cloned.1.call-start
  126.3 85.6 %reduce-scatter.3.cloned.1.call-done = f32[32,4096]{1,0:T(8,128)} async-done(((f32[32,65536]{1,0:T(8,128)}), f32[32,4096]{1,0:T(8,128)}) %reduce-scatter.3.cloned.1.call-update) | async-done | bytes 524304 | tf_op jit(solution)/shard_map/reduce_scatter | solution.py:37
  211.8 1.8 convert_element_type.14
  213.6 0.0 all-gather.5.cloned.1.call-update
  213.6 0.2 reduce-scatter.5.cloned.1.call-start
  213.9 51.6 %all-gather.5.cloned.1.call-done = bf16[32,65536]{1,0:T(8,128)(2,1)} async-done(((bf16[32,4096]{1,0:T(8,128)(2,1)}), bf16[32,65536]{1,0:T(8,128)(2,1)}) %all-gather.5.cloned.1.call-update) | async-done | bytes 4194320 | tf_op jit(solution)/shard_map/all_gather | solution.py:39
  265.6 4.9 %copy_bitcast_fusion.1 = bf16[32,512,128]{2,0,1:T(8,128)(2,1)} fusion(bf16[32,65536]{1,0:T(8,128)(2,1)} %all-gather.5.cloned.1.call-done), kind=kLoop, calls=%fused_computation.9 | loop fusion | bytes 8388608 | tf_op jit(solution)/shard_map/reshape | solution.py:40
  270.4 3.4 gather_fusion.1
  273.9 9.0 %broadcast_multiply_fusion = f32[384,32,128]{2,1,0:T(8,128)} fusion(f32[384]{0:T(512)S(1)} %get-tuple-element.6, bf16[1,1,384,128,128]{4,3,2,1,0:T(8,128)(2,1)} %param.5, bf16[384,32,128]{2,1,0:T(8,128)(2,1)S(1)} %gather_fusion.1, pred[384]{0:T(512)(128)(4,1)S(1)} %compare_and_fusion), kind=kOutput, calls=%fused_computation.14 | convolution fusion | flops 405798912 | bytes 22022016 | tf_op jit(solution)/shard_map/ksi,sij->ksj/dot_general | solution.py:45
  282.9 2.6 broadcast_in_dim.31
  285.5 51.3 %scatter_fusion.1 = f32[32,256,128]{2,0,1:T(8,128)} fusion(f32[32,256,128]{2,0,1:T(8,128)} %broadcast_in_dim.31, s32[384]{0:T(512)S(1)} %fusion.22, f32[384,32,128]{2,1,0:T(8,128)} %broadcast_multiply_fusion), kind=kCustom, calls=%fused_computation.3 | custom fusion | flops 1572864 | bytes 18875904 | tf_op jit(solution)/shard_map/scatter-add | solution.py:46
  336.8 6.5 %copy.22 = f32[32,256,128]{2,1,0:T(8,128)} copy(f32[32,256,128]{2,0,1:T(8,128)} %scatter_fusion.1) | data formatting | bytes 8388608 | tf_op jit(solution)/shard_map/scatter-add | solution.py:46
  343.3 5.0 %reshape.92 = f32[32,8,1,4096]{3,1,0,2:T(8,128)} reshape(f32[32,256,128]{2,1,0:T(8,128)} %copy.22) | data formatting | bytes 8388608 | tf_op jit(solution)/shard_map/reshape | solution.py:49
  348.3 6.5 %copy.23 = f32[32,8,1,4096]{3,0,2,1:T(8,128)} copy(f32[32,8,1,4096]{3,1,0,2:T(8,128)} %reshape.92) | data formatting | bytes 8388608 | tf_op jit(solution)/shard_map/reshape | solution.py:49
  354.9 37.6 %reduce-scatter.5.cloned.1.call-done = f32[32,1,1,4096]{3,0,2,1:T(8,128)} async-done(((f32[32,8,1,4096]{3,0,2,1:T(8,128)}), f32[32,1,1,4096]{3,0,2,1:T(8,128)}) %reduce-scatter.5.cloned.1.call-update) | async-done | bytes 524304 | tf_op jit(solution)/shard_map/reduce_scatter | solution.py:50
  392.5 1.8 convert_element_type.15
  (8 shorter events, 0.1 us)
Async XLA Ops:
  7.2 30.2 %all-gather.3.cloned.1.call-start = ((), (), s32[]{:S(2)}) async-start(), calls=%async_computation.2 | async-start | bytes 2359296 | tf_op jit(solution)/shard_map/all_gather | solution.py:18
  7.9 203.9 %reduce-scatter.3.cloned.1.call-start = ((), (), s32[]{:S(2)}) async-start(), calls=%async_computation.3 | async-start | bytes 8912896 | tf_op jit(solution)/shard_map/reduce_scatter | solution.py:37
  126.2 87.7 %copy-start = (s32[1,1,384]{2,1,0:T(1,128)S(1)}, s32[1,1,384]{2,1,0:T(1,128)}, u32[]{:S(2)}) copy-start(s32[1,1,384]{2,1,0:T(1,128)} %param.6) | copy-start | bytes 4612
  126.2 139.3 %all-gather.5.cloned.1.call-start = ((), (), s32[]{:S(2)}) async-start(), calls=%async_computation.4 | async-start | bytes 4456448 | tf_op jit(solution)/shard_map/all_gather | solution.py:39
  213.6 178.8 %reduce-scatter.5.cloned.1.call-start = ((), (), s32[]{:S(2)}) async-start(), calls=%async_computation.5 | async-start | bytes 4718592 | tf_op jit(solution)/shard_map/reduce_scatter | solution.py:50
Sparse Core Ops, SparseCore 0:
  9.7 27.5 all-gather.2
  126.3 85.4 reduce-scatter.2
  214.6 50.9 all-gather.4
  355.0 37.4 reduce-scatter.4
where the time goes:
time: 402 us; the launch traced here: 401 us
  waiting for transfers between devices  202 us (50%)
  other arithmetic  108 us (27%)
  local copies, waits for them, and re-layouts  51.6 us (13%)
  matrix products  24 us (6%)
  between operations  14.4 us (4%)
    reduce_scatter x1, waiting for transfers between devices, per_device(): lax.psum_scatter(partial_rows, 'col', scatter_dimension=1, tiled=True)  85.6 us
    all_gather x1, waiting for transfers between devices, per_device(): row_image = lax.all_gather(image, 'col', axis=1, tiled=True)  51.6 us
    scatter-add x1, other arithmetic, backward_terms(): return totals.at[:, col_index].add(product * slot_mask[None, :, None])  51.3 us
    scatter-add x1, other arithmetic, forward_terms(): return totals.at[:, row_index].add(product * slot_mask[None, :, None])  51.2 us
    reduce_scatter x1, waiting for transfers between devices, per_device(): lax.psum_scatter(partial_cols, 'row', scatter_dimension=1, tiled=True)  37.6 us
    all_gather x1, waiting for transfers between devices, per_device(): gathered = lax.all_gather(vectors, 'row', axis=1, tiled=True)  26.6 us
    dot_general x1, matrix products, forward_terms(): jnp.einsum('ksj,sij->ksi', picked, tile_block, preferred_element_type=jnp...  14.9 us
    reshape x2, local copies, waits for them, and re-layouts, per_device(): backward_sum.reshape(vec_cols, row_devices, 1, vectors.shape[3])  11.5 us
  transfers between devices with their start and end apart: 4, of which 4 were waited for; matrix products, arithmetic and copies ran while one was open for 1% of the time, Pallas kernels for 0%

commit v1 on v0

--- a/solution.py
+++ b/solution.py
@@ -36,7 +36,9 @@
     partial_rows = forward_sum.reshape(vec_cols, blk_rows * tile_size)
     share_sum = lax.psum_scatter(partial_rows, "col", scatter_dimension=1, tiled=True)
     image = share_sum.astype(jnp.bfloat16)
-    row_image = lax.all_gather(image, "col", axis=1, tiled=True)
+    row_image = jnp.concatenate(
+        lax.all_to_all(jnp.stack([image] * lax.axis_size("col")), "col", 0, 0), axis=1
+    )
     row_blocks = row_image.reshape(vec_cols, blk_rows, tile_size)
 
     def backward_terms(totals, start_slot, group_size):

time: 402 us -> 432 us (1.075)
  local copies, waits for them, and re-layouts: 51.6 us -> 69.9 us
  waiting for transfers between devices: 202 us -> 209 us
  starting transfers between devices: 0.34 us -> 5.48 us
    all_to_all x0 -> x1, waiting for transfers between devices: none -> 59.6 us  [per_device(): lax.all_to_all(jnp.stack([image] * lax.axis_size('col')), 'col', 0, 0)]
    all_gather x1 -> x0, waiting for transfers between devices: 51.6 us -> none  [per_device(): row_image = lax.all_gather(image, 'col', axis=1, tiled=True)]
    another operation x0 -> x3, local copies, waits for them, and re-layouts: none -> 16.7 us  [the longest x2 14.3 us: per_device(): row_blocks = row_image.reshape(vec_cols, blk_rows, tile_size)]
    all_to_all x0 -> x1, starting transfers between devices: none -> 5.18 us  [per_device(): lax.all_to_all(jnp.stack([image] * lax.axis_size('col')), 'col', 0, 0)]
  transfers between devices with their start and end apart: 4 -> 4, of which waited for: 4 -> 4; matrix products, arithmetic and copies ran while one was open for 1% -> 0% of each run, Pallas kernels for 0% -> 0%
where the time goes in v1:
time: 432 us; the launch traced here: 430 us
  waiting for transfers between devices  209 us (48%)
  other arithmetic  108 us (25%)
  local copies, waits for them, and re-layouts  69.9 us (16%)
  matrix products  24 us (6%)
  between operations  14.5 us (3%)
  starting transfers between devices  5.48 us (1%)
    reduce_scatter x1, waiting for transfers between devices, per_device(): lax.psum_scatter(partial_rows, 'col', scatter_dimension=1, tiled=True)  85.6 us
    all_to_all x1, waiting for transfers between devices, per_device(): lax.all_to_all(jnp.stack([image] * lax.axis_size('col')), 'col', 0, 0)  59.6 us
    scatter-add x1, other arithmetic, backward_terms(): return totals.at[:, col_index].add(product * slot_mask[None, :, None])  51.3 us
    scatter-add x1, other arithmetic, forward_terms(): return totals.at[:, row_index].add(product * slot_mask[None, :, None])  51.2 us
    reduce_scatter x1, waiting for transfers between devices, per_device(): lax.psum_scatter(partial_cols, 'row', scatter_dimension=1, tiled=True)  36 us
    all_gather x1, waiting for transfers between devices, per_device(): gathered = lax.all_gather(vectors, 'row', axis=1, tiled=True)  26.6 us
    dot_general x1, matrix products, forward_terms(): jnp.einsum('ksj,sij->ksi', picked, tile_block, preferred_element_type=jnp...  14.9 us
    another operation x2, local copies, waits for them, and re-layouts, per_device(): row_blocks = row_image.reshape(vec_cols, blk_rows, tile_size)  14.3 us
  transfers between devices with their start and end apart: 4, of which 4 were waited for; matrix products, arithmetic and copies ran while one was open for 0% of the time, Pallas kernels for 0%

profile of v1, /device:TPU:0, one launch (start us, length us, event | category | flops | bytes accessed | tf_op | source)
XLA Modules:
  0.0 430.0 jit_solution(8558869205527041036)
XLA Ops:
  7.2 0.7 all-gather.2.cloned.1.call-update
  7.9 0.0 reduce-scatter.3.cloned.1.call-start
  8.6 0.7 reduce.1
  9.3 0.7 fusion.22
  10.0 0.7 fusion.21
  10.7 26.6 %all-gather.2.cloned.1.call-done = bf16[32,8,1,4096]{3,0,2,1:T(8,128)(2,1)} async-done(((bf16[32,1,1,4096]{3,0,2,1:T(8,128)(2,1)}), bf16[32,8,1,4096]{3,0,2,1:T(8,128)(2,1)}) %all-gather.2.cloned.1.call-update) | async-done | bytes 2097168 | tf_op jit(solution)/shard_map/all_gather | solution.py:18
  37.3 2.7 copy.13
  40.1 2.4 reshape.91
  42.5 2.9 copy.14
  45.4 3.2 gather_fusion
  48.6 14.9 %broadcast_multiply_fusion.1 = f32[384,32,128]{2,1,0:T(8,128)} fusion(f32[384]{0:T(512)S(1)} %get-tuple-element.4, bf16[1,1,384,128,128]{4,3,2,1,0:T(8,128)(2,1)} %param.5, bf16[384,32,128]{2,1,0:T(8,128)(2,1)} %gather_fusion, pred[384]{0:T(512)(128)(4,1)S(1)} %get-tuple-element.5), kind=kOutput, calls=%fused_computation.14 | convolution fusion | flops 405798912 | bytes 22022016 | tf_op jit(solution)/shard_map/ksj,sij->ksi/dot_general | solution.py:29
  63.5 4.3 broadcast_in_dim.28
  67.8 51.2 %scatter_fusion = f32[32,512,128]{2,0,1:T(8,128)} fusion(f32[32,512,128]{2,0,1:T(8,128)} %broadcast_in_dim.28, s32[384]{0:T(512)S(1)} %fusion.21, f32[384,32,128]{2,1,0:T(8,128)} %broadcast_multiply_fusion.1), kind=kCustom, calls=%fused_computation.2 | custom fusion | flops 1572864 | bytes 18875904 | tf_op jit(solution)/shard_map/scatter-add | solution.py:30
  119.1 7.1 %copy_bitcast_fusion = f32[32,65536]{1,0:T(8,128)} fusion(f32[32,512,128]{2,0,1:T(8,128)} %scatter_fusion), kind=kLoop, calls=%fused_computation.8 | loop fusion | bytes 16777216 | tf_op jit(solution)/shard_map/reshape | solution.py:36
  126.2 85.6 %reduce-scatter.3.cloned.1.call-done = f32[32,4096]{1,0:T(8,128)} async-done(((f32[32,65536]{1,0:T(8,128)}), f32[32,4096]{1,0:T(8,128)}) %reduce-scatter.3.cloned.1.call-update) | async-done | bytes 524304 | tf_op jit(solution)/shard_map/reduce_scatter | solution.py:37
  211.8 1.1 convert_element_type.14
  212.9 2.5 stack.2
  215.4 5.2 %all-to-all-start = ((bf16[16,32,4096]{2,1,0:T(8,128)(2,1)}), bf16[16,32,4096]{2,1,0:T(8,128)(2,1)}, u32[]{:S(2)}, u32[]{:S(2)}) async-start(bf16[16,32,4096]{2,1,0:T(8,128)(2,1)} %stack.2), calls=%async_computation.1 | async-start | bytes 8388608 | tf_op jit(solution)/shard_map/all_to_all | solution.py:40
  220.6 0.2 reduce-scatter.5.cloned.1.call-start
  220.9 59.6 %all-to-all-done = bf16[16,32,4096]{2,1,0:T(8,128)(2,1)} async-done(((bf16[16,32,4096]{2,1,0:T(8,128)(2,1)}), bf16[16,32,4096]{2,1,0:T(8,128)(2,1)}, u32[]{:S(2)}, u32[]{:S(2)}) %all-to-all-start) | async-done | bytes 4194336 | tf_op jit(solution)/shard_map/all_to_all | solution.py:40
  280.5 6.5 %copy.16 = bf16[32,16,4096]{2,1,0:T(8,128)(2,1)} copy(bf16[32,16,4096]{2,0,1:T(8,128)(2,1)} %bitcast.5) | data formatting | bytes 8388608 | tf_op jit(solution)/shard_map/reshape | solution.py:39
  287.0 7.4 %reshape_reshape.3 = bf16[32,512,128]{2,1,0:T(8,128)(2,1)} reshape(bf16[32,16,4096]{2,1,0:T(8,128)(2,1)} %copy.16) | data formatting | bytes 8388608 | tf_op jit(solution)/shard_map/reshape;reshape | solution.py:42
  294.4 6.9 %copy.17 = bf16[32,512,128]{2,0,1:T(8,128)(2,1)} copy(bf16[32,512,128]{2,1,0:T(8,128)(2,1)} %reshape_reshape.3) | data formatting | bytes 8388608 | tf_op jit(solution)/shard_map/reshape;reshape | solution.py:42
  301.2 3.4 gather_fusion.1
  304.7 9.0 %broadcast_multiply_fusion = f32[384,32,128]{2,1,0:T(8,128)} fusion(f32[384]{0:T(512)S(1)} %get-tuple-element.4, bf16[1,1,384,128,128]{4,3,2,1,0:T(8,128)(2,1)} %param.5, bf16[384,32,128]{2,1,0:T(8,128)(2,1)S(1)} %gather_fusion.1, pred[384]{0:T(512)(128)(4,1)S(1)} %compare_and_fusion), kind=kOutput, calls=%fused_computation.13 | convolution fusion | flops 405798912 | bytes 22022016 | tf_op jit(solution)/shard_map/ksi,sij->ksj/dot_general | solution.py:47
  313.7 2.6 broadcast_in_dim.31
  316.3 51.3 %scatter_fusion.1 = f32[32,256,128]{2,0,1:T(8,128)} fusion(f32[32,256,128]{2,0,1:T(8,128)} %broadcast_in_dim.31, s32[384]{0:T(512)S(1)} %fusion.22, f32[384,32,128]{2,1,0:T(8,128)} %broadcast_multiply_fusion), kind=kCustom, calls=%fused_computation.3 | custom fusion | flops 1572864 | bytes 18875904 | tf_op jit(solution)/shard_map/scatter-add | solution.py:48
  367.6 6.5 %copy.18 = f32[32,256,128]{2,1,0:T(8,128)} copy(f32[32,256,128]{2,0,1:T(8,128)} %scatter_fusion.1) | data formatting | bytes 8388608 | tf_op jit(solution)/shard_map/scatter-add | solution.py:48
  374.1 5.0 %reshape.94 = f32[32,8,1,4096]{3,1,0,2:T(8,128)} reshape(f32[32,256,128]{2,1,0:T(8,128)} %copy.18) | data formatting | bytes 8388608 | tf_op jit(solution)/shard_map/reshape | solution.py:51
  379.1 6.5 %copy.19 = f32[32,8,1,4096]{3,0,2,1:T(8,128)} copy(f32[32,8,1,4096]{3,1,0,2:T(8,128)} %reshape.94) | data formatting | bytes 8388608 | tf_op jit(solution)/shard_map/reshape | solution.py:51
  385.6 36.0 %reduce-scatter.5.cloned.1.call-done = f32[32,1,1,4096]{3,0,2,1:T(8,128)} async-done(((f32[32,8,1,4096]{3,0,2,1:T(8,128)}), f32[32,1,1,4096]{3,0,2,1:T(8,128)}) %reduce-scatter.5.cloned.1.call-update) | async-done | bytes 524304 | tf_op jit(solution)/shard_map/reduce_scatter | solution.py:52
  421.7 1.8 convert_element_type.15
  (12 shorter events, 0.1 us)
Async XLA Ops:
  7.2 30.2 %all-gather.2.cloned.1.call-start = ((), (), s32[]{:S(2)}) async-start(), calls=%async_computation.3 | async-start | bytes 2359296 | tf_op jit(solution)/shard_map/all_gather | solution.py:18
  7.9 203.9 %reduce-scatter.3.cloned.1.call-start = ((), (), s32[]{:S(2)}) async-start(), calls=%async_computation.4 | async-start | bytes 8912896 | tf_op jit(solution)/shard_map/reduce_scatter | solution.py:37
  212.9 2.5 copy-start
  215.4 5.4 %copy-start.1 = (s32[1,1,384]{2,1,0:T(1,128)S(1)}, s32[1,1,384]{2,1,0:T(1,128)}, u32[]{:S(2)}) copy-start(s32[1,1,384]{2,1,0:T(1,128)} %param.6) | copy-start | bytes 4612
  215.4 65.1 %all-to-all-start = ((bf16[16,32,4096]{2,1,0:T(8,128)(2,1)}), bf16[16,32,4096]{2,1,0:T(8,128)(2,1)}, u32[]{:S(2)}, u32[]{:S(2)}) async-start(bf16[16,32,4096]{2,1,0:T(8,128)(2,1)} %stack.2), calls=%async_computation.1 | async-start | bytes 8388608 | tf_op jit(solution)/shard_map/all_to_all | solution.py:40
  220.6 201.1 %reduce-scatter.5.cloned.1.call-start = ((), (), s32[]{:S(2)}) async-start(), calls=%async_computation.5 | async-start | bytes 4718592 | tf_op jit(solution)/shard_map/reduce_scatter | solution.py:52
Sparse Core Ops, SparseCore 0:
  9.7 27.5 all-gather.1
  126.3 85.4 reduce-scatter.2
  385.8 35.8 reduce-scatter.4
